TPU v7x, 32 devices: a whole 2x2x4 slice. The times are simulated.
32 devices in a mesh: groups: 2 (over y), blk: 4 (over z), tile: 2 (over x), pair: 2 (over core).
Axes of the slice: x: 2, y: 2, z: 4, core: 2. Of those that a mesh axis runs over, the one named last changes fastest.
Arguments:
- left_tokens: bfloat16 [4, 1536, 768], P(('groups', 'pair'), 'blk', 'tile'), parts along dimension 0, may hold values from -32 to 32
- right_tokens: bfloat16 [4, 1536, 768], P(('groups', 'pair'), 'blk', 'tile'), parts along dimension 0, may hold values from -32 to 32
- self_qkv: bfloat16 [3, 768, 512], P(None, None, 'tile'), may hold values from -1 to 1
- self_out: bfloat16 [512, 768], P('tile'), may hold values from -0.25 to 0.25
- cross_qkv: bfloat16 [3, 768, 512], P(None, None, 'tile'), may hold values from -1 to 1
- cross_out: bfloat16 [512, 768], P('tile'), may hold values from -0.25 to 0.25
- reassemble: bfloat16 [768, 256], P('tile'), may hold values from -0.21875 to 0.21875
- conv_weight: bfloat16 [3, 3, 256, 256], replicated, may hold values from -0.125 to 0.125
Outputs:
- joined: bfloat16 [4, 12, 128, 256], P(('groups', 'pair'), 'blk', 'tile'), parts along dimension 0
There are 2 independent parts, one for each index of `groups`. A program takes and returns all parts, laid end to end along the dimension named above; an argument that names none is the same for every part. Nothing has to cross between parts.
All inputs are finite; a program needn't handle non-finite values.
Results may differ from a plain program's by a relative error of at most 0.018.
Values may be sent and summed in bfloat16 or wider, within the bound.
A program may use at most 64 MiB of HBM per device.

v0:
```python
import jax
import jax.numpy as jnp
from jax import lax
from jax.sharding import PartitionSpec as P

HD = 64
CH = 256
GRID_W = 128


def padded_2(cells, sides, width):
    for axis, dim in sides:
        count = lax.axis_size(axis)
        ends = count - 1
        head = lax.slice_in_dim(cells, 0, width, axis=dim)
        tail = lax.slice_in_dim(cells, cells.shape[dim] - width, cells.shape[dim], axis=dim)
        cells = jnp.concatenate(
            [
                lax.ppermute(tail, axis, [(i, (i + 1) % count) for i in range(ends)]),
                cells,
                lax.ppermute(head, axis, [((i + 1) % count, i) for i in range(ends)]),
            ],
            axis=dim,
        )
    return cells


def layer_norm(values):
    widened = values.astype(jnp.float32)
    centred = widened - jnp.mean(widened, axis=-1, keepdims=True)
    variance = jnp.mean(centred * centred, axis=-1, keepdims=True)
    return (centred * lax.rsqrt(variance + 1e-06)).astype(jnp.bfloat16)


def project_rows(normed, weight):
    return jnp.dot(normed, weight, preferred_element_type=jnp.float32).astype(jnp.bfloat16)


def initial_state(queries):
    query_count = queries.shape[0]
    head_count = queries.shape[1] // HD
    return (
        jnp.full((head_count, query_count), -1e30, jnp.float32),
        jnp.zeros((head_count, query_count), jnp.float32),
        jnp.zeros(queries.shape, jnp.float32),
    )


def attend_keys(running, queries, keys_rows, values_rows):
    maxima, totals, accumulated = running
    query_count = queries.shape[0]
    head_count = queries.shape[1] // HD
    key_count = keys_rows.shape[0]
    scores = jnp.einsum(
        "qhd,khd->hqk",
        queries.reshape(query_count, head_count, HD),
        keys_rows.reshape(key_count, head_count, HD),
        preferred_element_type=jnp.float32,
    ) * HD ** (-0.5)
    new_maxima = jnp.maximum(maxima, jnp.max(scores, axis=2))
    correction = jnp.exp(maxima - new_maxima)
    expanded = jnp.exp(scores - new_maxima[:, :, None])
    totals = totals * correction + jnp.sum(expanded, axis=2)
    mixed = jnp.einsum(
        "hqk,khd->qhd",
        expanded.astype(jnp.bfloat16),
        values_rows.reshape(key_count, head_count, HD),
        preferred_element_type=jnp.float32,
    )
    accumulated = (
        accumulated.reshape(query_count, head_count, HD) * correction.T[:, :, None] + mixed
    )
    return (new_maxima, totals, accumulated.reshape(query_count, head_count * HD))


def fold_keys(running, queries, keys_rows, values_rows):
    key_count = keys_rows.shape[0]
    block_rows = max((divisor for divisor in range(1, 1025) if key_count % divisor == 0))
    if block_rows == key_count:
        return attend_keys(running, queries, keys_rows, values_rows)
    stacked_keys = keys_rows.reshape(key_count // block_rows, block_rows, keys_rows.shape[1])
    stacked_values = values_rows.reshape(key_count // block_rows, block_rows, values_rows.shape[1])

    def step_block(current, blocks):
        return (attend_keys(current, queries, blocks[0], blocks[1]), None)

    result, unused = lax.scan(step_block, running, (stacked_keys, stacked_values))
    return result


def finish_state(running):
    maxima, totals, accumulated = running
    query_count = accumulated.shape[0]
    head_count = accumulated.shape[1] // HD
    normalized = accumulated.reshape(query_count, head_count, HD) / totals.T[:, :, None]
    return normalized.reshape(query_count, head_count * HD).astype(jnp.bfloat16)


def body(
    left_tokens, right_tokens, self_qkv, self_out, cross_qkv, cross_out, reassemble, conv_weight
):
    tiles = lax.axis_size("tile")
    tile_index = lax.axis_index("tile")
    token_count, feature_share = (left_tokens.shape[1], left_tokens.shape[2])
    packed = jnp.concatenate(
        [left_tokens[0].reshape(-1), right_tokens[0].reshape(-1), reassemble.reshape(-1)]
    )
    gathered = lax.all_gather(packed, "tile", axis=0)
    block = token_count * feature_share

    def features(offset):
        return jnp.concatenate(
            [
                gathered[i, offset : offset + block].reshape(token_count, feature_share)
                for i in range(tiles)
            ],
            axis=1,
        )

    left_full = features(0)
    right_full = features(block)
    reassemble_full = gathered[:, 2 * block :].reshape(tiles * reassemble.shape[0], CH)
    left_normed = layer_norm(left_full)
    right_normed = layer_norm(right_full)
    self_query = project_rows(left_normed, self_qkv[0])
    projected = jnp.stack(
        [
            project_rows(left_normed, self_qkv[1]),
            project_rows(left_normed, self_qkv[2]),
            project_rows(right_normed, cross_qkv[1]),
            project_rows(right_normed, cross_qkv[2]),
        ]
    )
    pieces = lax.all_gather(projected, "blk", axis=1, tiled=True)
    self_state = fold_keys(initial_state(self_query), self_query, pieces[0], pieces[1])
    self_mixed = finish_state(self_state)
    self_term = jnp.dot(self_mixed, self_out, preferred_element_type=jnp.float32)
    self_sum = lax.psum(self_term.astype(jnp.bfloat16), "tile").astype(jnp.float32)
    updated = (left_full.astype(jnp.float32) + self_sum).astype(jnp.bfloat16)
    updated_normed = layer_norm(updated)
    cross_query = project_rows(updated_normed, cross_qkv[0])
    cross_state = fold_keys(initial_state(cross_query), cross_query, pieces[2], pieces[3])
    cross_mixed = finish_state(cross_state)
    cross_term = jnp.dot(cross_mixed, cross_out, preferred_element_type=jnp.float32)
    cross_sum = lax.psum(cross_term.astype(jnp.bfloat16), "tile").astype(jnp.float32)
    final_tokens = (updated.astype(jnp.float32) + cross_sum).astype(jnp.bfloat16)
    band_rows = token_count // GRID_W
    column_count = GRID_W // tiles
    grid = jnp.pad(final_tokens.reshape(band_rows, GRID_W, -1), ((0, 0), (1, 1), (0, 0)))
    window = lax.dynamic_slice_in_dim(grid, tile_index * column_count, column_count + 2, axis=1)
    wide_map = (
        jnp.dot(
            window.reshape(band_rows * (column_count + 2), -1),
            reassemble_full,
            preferred_element_type=jnp.float32,
        )
        .astype(jnp.bfloat16)
        .reshape(band_rows, column_count + 2, CH)
    )
    feature_map = wide_map[:, 1 : column_count + 1]
    activated = jnp.maximum(wide_map, jnp.zeros((), jnp.bfloat16))
    padded = padded_2(activated, (("blk", 0),), 1)
    stacked = jnp.concatenate(
        [
            padded[row_shift : row_shift + band_rows, col_shift : col_shift + column_count]
            for row_shift in range(3)
            for col_shift in range(3)
        ],
        axis=-1,
    )
    convolved = jnp.dot(
        stacked.reshape(band_rows * column_count, 9 * CH),
        conv_weight.reshape(9 * CH, CH),
        preferred_element_type=jnp.float32,
    )
    joined = (
        feature_map.astype(jnp.float32) + convolved.reshape(band_rows, column_count, CH)
    ).astype(jnp.bfloat16)
    return joined[None]


def solution(mesh):
    placed = (
        P(("groups", "pair"), "blk", "tile"),
        P(("groups", "pair"), "blk", "tile"),
        P(None, None, "tile"),
        P("tile", None),
        P(None, None, "tile"),
        P("tile", None),
        P("tile", None),
        P(),
    )
    return jax.shard_map(
        body,
        mesh=mesh,
        in_specs=placed,
        out_specs=P(("groups", "pair"), "blk", "tile", None),
        check_vma=False,
    )
```

profile of v0, /device:TPU:0, one launch (start us, length us, event | category | flops | bytes accessed | tf_op | source)
XLA Modules:
  0.0 234.0 jit_solution(1149109852763883605)
XLA Ops:
  6.5 1.2 copy.31
  7.7 1.1 reshape_squeeze.30
  9.0 0.9 pad_maximum_fusion
  10.0 30.0 %all-gather.6.cloned.1.call-done = bf16[786432]{0:T(1024)(128)(2,1)} async-done(((bf16[393216]{0:T(1024)(128)(2,1)}), bf16[786432]{0:T(1024)(128)(2,1)}) %all-gather.6.cloned.1.call-update) | async-done | bytes 1572880 | tf_op jit(solution)/shard_map/all_gather | solution.py:108
  40.0 1.8 reshape.110
  41.9 7.2 %slice_reduce_fusion.3 = (bf16[147456]{0:T(1024)(128)(2,1)S(1)}, bf16[147456]{0:T(1024)(128)(2,1)}, bf16[147456]{0:T(1024)(128)(2,1)}, bf16[147456]{0:T(1024)(128)(2,1)S(1)}) fusion(bf16[2,393216]{1,0:T(2,128)(2,1)S(1)} %reshape.110), kind=kLoop, calls=%fused_computation.80 | loop fusion | bytes 2359296 | tf_op jit(solution)/shard_map/slice | solution.py:114
  49.0 1.1 reshape_squeeze.35
  50.1 1.1 reshape_squeeze.34
  51.4 0.3 fusion.42
  51.7 1.4 fusion.49
  53.1 1.4 fusion.48
  55.0 0.3 fusion.40
  55.3 0.2 fusion.41
  55.6 0.6 copy-done.13
  56.2 0.3 fusion.47
  56.5 0.3 fusion.46
  56.9 1.0 pad_maximum_fusion.1
  57.9 1.3 convolution_convert_fusion.3
  59.4 62.0 %all-gather.4.cloned.1.call-done = bf16[4,1536,256]{2,1,0:T(8,128)(2,1)} async-done(((bf16[4,384,256]{2,1,0:T(8,128)(2,1)}), bf16[4,1536,256]{2,1,0:T(8,128)(2,1)}) %all-gather.4.cloned.1.call-update) | async-done | bytes 3145744 | tf_op jit(solution)/shard_map/all_gather | solution.py:134
  121.5 3.3 %fusion.82 = (bf16[1,1536,256]{2,1,0:T(8,128)(2,1)S(1)}, bf16[1,1536,256]{2,1,0:T(8,128)(2,1)}, bf16[1,1536,256]{2,1,0:T(8,128)(2,1)}, bf16[1,1536,256]{2,1,0:T(8,128)(2,1)}) fusion(bf16[4,1536,256]{2,1,0:T(8,128)(2,1)} %all-gather.4.cloned.1.call-done), kind=kLoop, calls=%fused_computation.131 | loop fusion | bytes 6291456 | tf_op jit(solution)/shard_map/slice | solution.py:142
  124.8 11.9 %while.30 = (s32[]{:T(128)}, f32[4,384]{1,0:T(4,128)S(1)}, f32[4,384]{1,0:T(4,128)S(1)}, f32[384,256]{0,1:T(8,128)S(1)}, bf16[2,768,256]{2,1,0:T(8,128)(2,1)}, /...) while((s32[]{:T(128)}, f32[4,384]{1,0:T(4,128)S(1)}, ...), condition=%wide.region_7.8_spmd.clone, body=%wide.region_4.7_spmd.clone.sunk | while | flops 311632896 | bytes 20742316 | solution.py:87
  124.8 0.7 copy-done.6
  125.5 1.2 constant_dynamic-slice_fusion.6
  126.7 0.2 copy.36
  126.8 0.2 copy.37
  127.0 1.8 bitcast_reduce_fusion.4
  128.8 1.0 fusion.124
  129.8 0.8 fusion.122
  130.7 0.7 copy-done.6
  131.4 1.2 constant_dynamic-slice_fusion.6
  132.6 0.2 copy.36
  132.9 1.8 bitcast_reduce_fusion.4
  134.7 1.0 fusion.124
  135.8 0.8 fusion.122
  136.7 2.2 convolution_convert_fusion.1
  139.0 0.2 all-reduce.6.cloned.1.call-start
  139.2 28.6 %all-reduce.4.cloned.1.call-done = bf16[384,768]{1,0:T(8,128)(2,1)} async-done(((bf16[384,768]{1,0:T(8,128)(2,1)}), bf16[384,768]{1,0:T(8,128)(2,1)}) %all-reduce.4.cloned.1.call-update) | async-done | bytes 589840 | tf_op jit(solution)/shard_map/psum | solution.py:138
  167.8 1.3 convert_reduce_fusion
  169.2 0.3 fusion.38
  169.5 1.4 convolution_convert_fusion.2
  171.1 11.6 %while.31 = (s32[]{:T(128)}, f32[4,384]{1,0:T(4,128)S(1)}, f32[4,384]{1,0:T(4,128)S(1)}, f32[384,256]{0,1:T(8,128)S(1)}, bf16[2,768,256]{2,1,0:T(8,128)(2,1)}, /...) while((s32[]{:T(128)}, f32[4,384]{1,0:T(4,128)S(1)}, ...), condition=%wide.region_14.15_spmd.clone, body=%wide.region_11.14_spmd.clone.sunk | while | flops 311632896 | bytes 20742316 | solution.py:87
  171.1 0.7 copy-done.8
  171.8 1.0 constant_dynamic-slice_fusion.7
  172.8 0.2 copy.38
  173.0 0.2 copy.39
  173.2 1.8 bitcast_reduce_fusion.5
  175.0 1.0 fusion.132
  176.0 0.8 fusion.130
  176.9 0.7 copy-done.8
  177.6 1.0 constant_dynamic-slice_fusion.7
  178.6 0.2 copy.38
  179.0 1.8 bitcast_reduce_fusion.5
  180.8 1.0 fusion.132
  181.8 0.8 fusion.130
  182.8 2.3 convolution_convert_fusion
  185.1 0.2 reshape.107
  185.3 30.0 %all-reduce.6.cloned.1.call-done = bf16[384,768]{1,0:T(8,128)(2,1)} async-done(((bf16[384,768]{1,0:T(8,128)(2,1)}), bf16[384,768]{1,0:T(8,128)(2,1)}) %all-reduce.6.cloned.1.call-update) | async-done | bytes 589840 | tf_op jit(solution)/shard_map/psum | solution.py:145
  215.3 1.2 fusion.45
  216.7 0.3 convolution_convert_fusion.8
  217.0 3.4 %collective-permute-start = (bf16[1,66,256]{2,1,0:T(8,128)(2,1)S(1)}, bf16[1,66,256]{2,1,0:T(8,128)(2,1)S(1)}, u32[]{:S(2)}, u32[]{:S(2)}) collective-permute-start(bf16[1,66,256]{2,1,0:T(8,128)(2,1)S(1)} %get-tuple-element.212), channel_id=1, source_target_pairs={{0,4},{4,8},{8,12},{1,5},{5,9},{9,13},{2,6},{6,10},{10,14},{3,7},{... | collective-permute-start | bytes 101384 | tf_op jit(solution)/shard_map/ppermute | solution.py:19
  220.4 1.3 collective-permute-start.1
  221.7 0.3 collective-permute-done
  222.2 4.1 %collective-permute-done.1 = bf16[1,66,256]{2,1,0:T(8,128)(2,1)S(1)} collective-permute-done((bf16[1,66,256]{2,1,0:T(8,128)(2,1)S(1)}, bf16[1,66,256]{2,1,0:T(8,128)(2,1)S(1)}, u32[]{:S(2)}, u32[]{:S(2)}) %collective-permute-start.1) | collective-permute-done | bytes 33824 | tf_op jit(solution)/shard_map/ppermute | solution.py:21
  226.4 1.1 fusion.51
  (89 shorter events, 2.8 us)
Async XLA Ops:
  6.5 219.8 %copy-start = (bf16[3,3,256,256]{3,2,1,0:T(8,128)(2,1)S(1)}, bf16[3,3,256,256]{3,2,1,0:T(8,128)(2,1)}, u32[]{:S(2)}) copy-start(bf16[3,3,256,256]{3,2,1,0:T(8,128)(2,1)} %param.19) | copy-start | bytes 3538948
  6.5 2.3 copy-start.12
  6.5 33.5 %all-gather.6.cloned.1.call-start = ((), (), s32[]{:S(2)}) async-start(), calls=%async_computation.3 | async-start | bytes 2359296 | tf_op jit(solution)/shard_map/all_gather | solution.py:108
  10.0 111.5 %all-gather.4.cloned.1.call-start = ((), (), s32[]{:S(2)}) async-start(), calls=%async_computation | async-start | bytes 3932160 | tf_op jit(solution)/shard_map/all_gather | solution.py:134
  41.8 7.2 %copy-start.1 = (bf16[2,393216]{1,0:T(2,128)(2,1)}, bf16[2,393216]{1,0:T(2,128)(2,1)S(1)}, u32[]{:S(2)}) copy-start(bf16[2,393216]{1,0:T(2,128)(2,1)S(1)} %reshape.110) | copy-start | bytes 4718596
  54.7 0.9 copy-start.2
  54.8 0.8 copy-start.4
  54.8 1.4 copy-start.13
  57.9 110.0 %all-reduce.4.cloned.1.call-start = ((), (), s32[]{:S(2)}) async-start(), calls=%async_computation.1 | async-start | bytes 1179648 | tf_op jit(solution)/shard_map/psum | solution.py:138
  124.8 0.7 copy-start.6
  129.8 0.9 copy-start.7
  130.7 0.7 copy-start.6
  135.7 0.9 copy-start.7
  136.7 31.2 %copy-start.3 = (bf16[384,384]{1,0:T(8,128)(2,1)S(1)}, bf16[384,384]{1,0:T(8,128)(2,1)}, u32[]{:S(2)}) copy-start(bf16[384,384]{1,0:T(8,128)(2,1)} %copy-done.2) | copy-start | bytes 884740
  136.7 31.2 %copy-start.5 = (bf16[384,384]{1,0:T(8,128)(2,1)S(1)}, bf16[384,384]{1,0:T(8,128)(2,1)}, u32[]{:S(2)}) copy-start(bf16[384,384]{1,0:T(8,128)(2,1)} %copy-done.4) | copy-start | bytes 884740
  139.0 76.3 %all-reduce.6.cloned.1.call-start = ((), (), s32[]{:S(2)}) async-start(), calls=%async_computation.2 | async-start | bytes 1179648 | tf_op jit(solution)/shard_map/psum | solution.py:145
  169.2 1.7 copy-start.10
  171.1 0.7 copy-start.8
  176.0 0.9 copy-start.9
  176.9 0.7 copy-start.8
  181.8 0.9 copy-start.9
  182.8 2.3 slice-start
  185.0 30.3 %copy-start.11 = (bf16[384,768]{1,0:T(8,128)(2,1)S(1)}, bf16[384,768]{1,0:T(8,128)(2,1)}, u32[]{:S(2)}) copy-start(bf16[384,768]{1,0:T(8,128)(2,1)} %copy-done.10) | copy-start | bytes 1769476
  217.0 5.0 %collective-permute-start = (bf16[1,66,256]{2,1,0:T(8,128)(2,1)S(1)}, bf16[1,66,256]{2,1,0:T(8,128)(2,1)S(1)}, u32[]{:S(2)}, u32[]{:S(2)}) collective-permute-start(bf16[1,66,256]{2,1,0:T(8,128)(2,1)S(1)} %get-tuple-element.212), channel_id=1, source_target_pairs={{0,4},{4,8},{8,12},{1,5},{5,9},{9,13},{2,6},{6,10},{10,14},{3,7},{... | collective-permute-start | bytes 101384 | tf_op jit(solution)/shard_map/ppermute | solution.py:19
  220.4 5.9 %collective-permute-start.1 = (bf16[1,66,256]{2,1,0:T(8,128)(2,1)S(1)}, bf16[1,66,256]{2,1,0:T(8,128)(2,1)S(1)}, u32[]{:S(2)}, u32[]{:S(2)}) collective-permute-start(bf16[1,66,256]{2,1,0:T(8,128)(2,1)S(1)} %get-tuple-element.211), channel_id=1, source_target_pairs={{4,0},{8,4},{12,8},{5,1},{9,5},{13,9},{6,2},{10,6},{14,10},{7,3},{... | collective-permute-start | bytes 101384 | tf_op jit(solution)/shard_map/ppermute | solution.py:21
Sparse Core Ops, SparseCore 0:
  10.1 29.8 all-gather.5
  58.0 63.4 all-gather.3
  139.1 28.7 all-reduce.3
  185.2 30.0 all-reduce.5
where the time goes:
time: 235 us; the launch traced here: 234 us
  waiting for transfers between devices  155 us (66%)
  local copies, waits for them, and re-layouts  27.7 us (12%)
  matrix products  23 us (10%)
  between operations  13.5 us (6%)
  other arithmetic  9.46 us (4%)
  starting transfers between devices  4.99 us (2%)
    all_gather x1, waiting for transfers between devices, body(): pieces = lax.all_gather(projected, 'blk', axis=1, tiled=True)  62 us
    all_gather x1, waiting for transfers between devices, body(): gathered = lax.all_gather(packed, 'tile', axis=0)  30 us
    psum x1, waiting for transfers between devices, body(): lax.psum(cross_term.astype(jnp.bfloat16), 'tile').astype(jnp.float32)  30 us
    psum x1, waiting for transfers between devices, body(): lax.psum(self_term.astype(jnp.bfloat16), 'tile').astype(jnp.float32)  28.6 us
    slice x1, local copies, waits for them, and re-layouts, features(): gathered[i, offset:offset + block].reshape(token_count, feature_share)  7.18 us
    dot_general x4, matrix products, attend_keys(): jnp.einsum('qhd,khd->hqk', queries.reshape(query_count, head_count, HD),...  7.05 us
    dot_general x6, matrix products, project_rows(): jnp.dot(normed, weight, preferred_element_type=jnp.float32)  6.08 us
    dynamic_slice x12, local copies, waits for them, and re-layouts, fold_keys(): lax.scan(step_block, running, (stacked_keys, stacked_values))  5.79 us
  transfers between devices with their start and end apart: 6, of which 6 were waited for; matrix products, arithmetic and copies ran while one was open for 1% of the time, Pallas kernels for 0%

commit v1 on v0

--- a/solution.py
+++ b/solution.py
@@ -6,6 +6,30 @@
 HD = 64
 CH = 256
 GRID_W = 128
+
+
+def register_surface(target, array_dim):
+    aux = list(target.shape[1:])
+    aux[array_dim] *= target.shape[0]
+    return jnp.moveaxis(target, 0, array_dim).reshape(aux)
+
+
+def classes_list(unit, named_axis):
+    reply = jax.lax.axis_index(named_axis)
+    block_now = jax.lax.axis_size(named_axis)
+    big, tall = (block_now, reply)
+    inter, arr_next = (unit[None], 1)
+    while arr_next < big:
+        tile_out = range(big)
+        finding = jax.lax.ppermute(
+            inter, axis_name=named_axis, perm=list(map(lambda at: (at, at ^ arr_next), tile_out))
+        )
+        z_new = tall & arr_next == 0
+        new = jnp.where(z_new, inter, finding)
+        met_up = jnp.where(z_new, finding, inter)
+        inter = jnp.concatenate([new, met_up])
+        arr_next *= 2
+    return inter
 
 
 def padded_2(cells, sides, width):
@@ -131,7 +155,8 @@
             project_rows(right_normed, cross_qkv[2]),
         ]
     )
-    pieces = lax.all_gather(projected, "blk", axis=1, tiled=True)
+    out_arr = classes_list(projected, "blk")
+    pieces = register_surface(out_arr, 1)
     self_state = fold_keys(initial_state(self_query), self_query, pieces[0], pieces[1])
     self_mixed = finish_state(self_state)
     self_term = jnp.dot(self_mixed, self_out, preferred_element_type=jnp.float32)

time: 235 us -> 264 us (1.12)
  waiting for transfers between devices: 155 us -> 178 us
  starting transfers between devices: 4.99 us -> 8.86 us
  other arithmetic: 9.46 us -> 13.2 us
    ppermute x0 -> x2, waiting for transfers between devices: none -> 83.9 us  [classes_list(): jax.lax.ppermute(inter, axis_name=named_axis, perm=list(map(lambda at: (a...]
    all_gather x1 -> x0, waiting for transfers between devices: 62 us -> none  [body(): pieces = lax.all_gather(projected, 'blk', axis=1, tiled=True)]
    ppermute x0 -> x2, starting transfers between devices: none -> 3.91 us  [classes_list(): jax.lax.ppermute(inter, axis_name=named_axis, perm=list(map(lambda at: (a...]
    select_n x0 -> x2, other arithmetic: none -> 3.09 us  [classes_list(): new = jnp.where(z_new, inter, finding)]
  transfers between devices with their start and end apart: 6 -> 7, of which waited for: 6 -> 7; matrix products, arithmetic and copies ran while one was open for 1% -> 1% of each run, Pallas kernels for 0% -> 0%
where the time goes in v1:
time: 264 us; the launch traced here: 263 us
  waiting for transfers between devices  178 us (67%)
  local copies, waits for them, and re-layouts  26.1 us (10%)
  matrix products  22.9 us (9%)
  between operations  13.5 us (5%)
  other arithmetic  13.2 us (5%)
  starting transfers between devices  8.86 us (3%)
    ppermute x2, waiting for transfers between devices, classes_list(): jax.lax.ppermute(inter, axis_name=named_axis, perm=list(map(lambda at: (a...  83.9 us
    all_gather x1, waiting for transfers between devices, body(): gathered = lax.all_gather(packed, 'tile', axis=0)  30 us
    psum x1, waiting for transfers between devices, body(): lax.psum(self_term.astype(jnp.bfloat16), 'tile').astype(jnp.float32)  30 us
    psum x1, waiting for transfers between devices, body(): lax.psum(cross_term.astype(jnp.bfloat16), 'tile').astype(jnp.float32)  30 us
    slice x1, local copies, waits for them, and re-layouts, features(): gathered[i, offset:offset + block].reshape(token_count, feature_share)  7.19 us
    dot_general x4, matrix products, attend_keys(): jnp.einsum('qhd,khd->hqk', queries.reshape(query_count, head_count, HD),...  7.05 us
    dot_general x6, matrix products, project_rows(): jnp.dot(normed, weight, preferred_element_type=jnp.float32)  6.07 us
    dynamic_slice x12, local copies, waits for them, and re-layouts, fold_keys(): lax.scan(step_block, running, (stacked_keys, stacked_values))  5.79 us
  transfers between devices with their start and end apart: 7, of which 7 were waited for; matrix products, arithmetic and copies ran while one was open for 1% of the time, Pallas kernels for 0%

profile of v1, /device:TPU:0, one launch (start us, length us, event | category | flops | bytes accessed | tf_op | source)
XLA Modules:
  0.0 263.2 jit_solution(10436239818872464787)
XLA Ops:
  6.5 1.2 copy.31
  7.7 1.1 reshape_squeeze.30
  9.0 1.0 pad_maximum_fusion.1
  10.0 30.0 %all-gather.3.cloned.1.call-done = bf16[786432]{0:T(1024)(128)(2,1)} async-done(((bf16[393216]{0:T(1024)(128)(2,1)}), bf16[786432]{0:T(1024)(128)(2,1)}) %all-gather.3.cloned.1.call-update) | async-done | bytes 1572880 | tf_op jit(solution)/shard_map/all_gather | solution.py:132
  40.0 1.8 reshape.119
  41.9 7.2 %slice_reduce_fusion.3 = (bf16[147456]{0:T(1024)(128)(2,1)S(1)}, bf16[147456]{0:T(1024)(128)(2,1)}, bf16[147456]{0:T(1024)(128)(2,1)}, bf16[147456]{0:T(1024)(128)(2,1)S(1)}) fusion(bf16[2,393216]{1,0:T(2,128)(2,1)S(1)} %reshape.119), kind=kLoop, calls=%fused_computation.86 | loop fusion | bytes 2359296 | tf_op jit(solution)/shard_map/slice | solution.py:138
  49.1 1.1 reshape_squeeze.35
  50.2 1.1 reshape_squeeze.34
  51.4 0.3 fusion.42
  51.8 1.4 fusion.49
  53.1 1.4 fusion.48
  55.0 0.3 fusion.40
  55.4 0.2 fusion.41
  55.6 0.6 copy-done.18
  56.2 0.3 fusion.47
  56.6 0.3 fusion.46
  57.2 1.5 collective-permute-start
  58.7 17.7 %collective-permute-done = bf16[1,4,384,256]{3,2,1,0:T(8,128)(2,1)} collective-permute-done((bf16[1,4,384,256]{3,2,1,0:T(8,128)(2,1)S(1)}, bf16[1,4,384,256]{3,2,1,0:T(8,128)(2,1)}, u32[]{:S(2)}, u32[]{:S(2)}) %collective-permute-start) | collective-permute-done | bytes 786464 | tf_op jit(solution)/shard_map/ppermute | solution.py:24
  76.5 1.5 broadcast_select_fusion.3
  78.0 1.3 pad_maximum_fusion
  79.2 2.4 collective-permute-start.1
  81.7 1.3 convolution_convert_fusion.3
  83.1 66.1 %collective-permute-done.1 = bf16[2,4,384,256]{3,2,1,0:T(8,128)(2,1)} collective-permute-done((bf16[2,4,384,256]{3,2,1,0:T(8,128)(2,1)}, bf16[2,4,384,256]{3,2,1,0:T(8,128)(2,1)}, u32[]{:S(2)}, u32[]{:S(2)}) %collective-permute-start.1) | collective-permute-done | bytes 1572896 | tf_op jit(solution)/shard_map/ppermute | solution.py:24
  149.3 1.6 broadcast_select_fusion.1
  150.9 0.3 maximum_bitcast_fusion
  151.2 1.4 fusion.82
  152.6 11.9 %while.30 = (s32[]{:T(128)}, f32[4,384]{1,0:T(4,128)S(1)}, f32[4,384]{1,0:T(4,128)S(1)}, f32[384,256]{0,1:T(8,128)S(1)}, bf16[2,768,256]{2,1,0:T(8,128)(2,1)}, /...) while((s32[]{:T(128)}, f32[4,384]{1,0:T(4,128)S(1)}, ...), condition=%wide.region_7.8_spmd.clone, body=%wide.region_4.7_spmd.clone.sunk | while | flops 311632896 | bytes 20742316 | solution.py:111
  152.7 0.7 copy-done.6
  153.3 1.2 constant_dynamic-slice_fusion.6
  154.9 1.8 bitcast_reduce_fusion.4
  156.6 1.0 fusion.124
  157.7 0.8 fusion.122
  158.6 0.7 copy-done.6
  159.3 1.2 constant_dynamic-slice_fusion.6
  160.8 1.8 bitcast_reduce_fusion.4
  162.6 1.0 fusion.124
  163.6 0.8 fusion.122
  164.6 2.2 convolution_convert_fusion.1
  166.8 0.2 all-reduce.6.cloned.1.call-start
  167.1 30.0 %all-reduce.4.cloned.1.call-done = bf16[384,768]{1,0:T(8,128)(2,1)} async-done(((bf16[384,768]{1,0:T(8,128)(2,1)}), bf16[384,768]{1,0:T(8,128)(2,1)}) %all-reduce.4.cloned.1.call-update) | async-done | bytes 589840 | tf_op jit(solution)/shard_map/psum | solution.py:163
  197.1 1.3 convert_reduce_fusion
  198.4 0.3 fusion.38
  198.7 1.4 convolution_convert_fusion.2
  200.3 11.7 %while.31 = (s32[]{:T(128)}, f32[4,384]{1,0:T(4,128)S(1)}, f32[4,384]{1,0:T(4,128)S(1)}, f32[384,256]{0,1:T(8,128)S(1)}, bf16[2,768,256]{2,1,0:T(8,128)(2,1)}, /...) while((s32[]{:T(128)}, f32[4,384]{1,0:T(4,128)S(1)}, ...), condition=%wide.region_14.15_spmd.clone, body=%wide.region_11.14_spmd.clone.sunk | while | flops 311632896 | bytes 20742316 | solution.py:111
  200.3 0.7 copy-done.8
  201.0 1.0 constant_dynamic-slice_fusion.7
  202.4 1.8 bitcast_reduce_fusion.5
  204.2 1.0 fusion.132
  205.2 0.8 fusion.130
  206.2 0.7 copy-done.8
  206.9 1.0 constant_dynamic-slice_fusion.7
  208.3 1.8 bitcast_reduce_fusion.5
  210.1 1.0 fusion.132
  211.1 0.8 fusion.130
  212.1 2.2 convolution_convert_fusion
  214.3 0.2 reshape.116
  214.6 30.0 %all-reduce.6.cloned.1.call-done = bf16[384,768]{1,0:T(8,128)(2,1)} async-done(((bf16[384,768]{1,0:T(8,128)(2,1)}), bf16[384,768]{1,0:T(8,128)(2,1)}) %all-reduce.6.cloned.1.call-update) | async-done | bytes 589840 | tf_op jit(solution)/shard_map/psum | solution.py:170
  244.6 1.2 fusion.45
  246.0 0.3 convolution_convert_fusion.8
  246.3 3.4 %collective-permute-start.2 = (bf16[1,66,256]{2,1,0:T(8,128)(2,1)S(1)}, bf16[1,66,256]{2,1,0:T(8,128)(2,1)S(1)}, u32[]{:S(2)}, u32[]{:S(2)}) collective-permute-start(bf16[1,66,256]{2,1,0:T(8,128)(2,1)S(1)} %get-tuple-element.216), channel_id=1, source_target_pairs={{0,4},{4,8},{8,12},{1,5},{5,9},{9,13},{2,6},{6,10},{10,14},{3,7},{... | collective-permute-start | bytes 101384 | tf_op jit(solution)/shard_map/ppermute | solution.py:43
  249.7 1.3 collective-permute-start.3
  251.0 0.3 collective-permute-done.2
  251.5 4.1 %collective-permute-done.3 = bf16[1,66,256]{2,1,0:T(8,128)(2,1)S(1)} collective-permute-done((bf16[1,66,256]{2,1,0:T(8,128)(2,1)S(1)}, bf16[1,66,256]{2,1,0:T(8,128)(2,1)S(1)}, u32[]{:S(2)}, u32[]{:S(2)}) %collective-permute-start.3) | collective-permute-done | bytes 33824 | tf_op jit(solution)/shard_map/ppermute | solution.py:45
  255.6 1.1 fusion.51
  (104 shorter events, 4.0 us)
Async XLA Ops:
  6.5 249.1 %copy-start = (bf16[3,3,256,256]{3,2,1,0:T(8,128)(2,1)S(1)}, bf16[3,3,256,256]{3,2,1,0:T(8,128)(2,1)}, u32[]{:S(2)}) copy-start(bf16[3,3,256,256]{3,2,1,0:T(8,128)(2,1)} %param.19) | copy-start | bytes 3538948
  6.5 2.3 copy-start.17
  6.5 33.5 %all-gather.3.cloned.1.call-start = ((), (), s32[]{:S(2)}) async-start(), calls=%async_computation.2 | async-start | bytes 2359296 | tf_op jit(solution)/shard_map/all_gather | solution.py:132
  10.0 187.1 %all-reduce.4.cloned.1.call-start = ((), (), s32[]{:S(2)}) async-start(), calls=%async_computation | async-start | bytes 1179648 | tf_op jit(solution)/shard_map/psum | solution.py:163
  41.9 7.2 %copy-start.1 = (bf16[2,393216]{1,0:T(2,128)(2,1)}, bf16[2,393216]{1,0:T(2,128)(2,1)S(1)}, u32[]{:S(2)}) copy-start(bf16[2,393216]{1,0:T(2,128)(2,1)S(1)} %reshape.119) | copy-start | bytes 4718596
  54.5 2.4 copy-start.12
  54.7 0.9 copy-start.2
  54.8 0.8 copy-start.4
  54.8 1.4 copy-start.18
  56.2 0.8 copy-start.15
  56.6 0.7 copy-start.13
  57.1 1.7 copy-start.14
  57.2 19.2 %collective-permute-start = (bf16[1,4,384,256]{3,2,1,0:T(8,128)(2,1)S(1)}, bf16[1,4,384,256]{3,2,1,0:T(8,128)(2,1)}, u32[]{:S(2)}, u32[]{:S(2)}) collective-permute-start(bf16[1,4,384,256]{3,2,1,0:T(8,128)(2,1)S(1)} %maximum_bitcast_fusion.1), channel_id=1, source_target_pairs={{0,4},{4,0},{8,12},{12,8},{1,5},{5,1},{9,13},{13,9},{2,6},{6,2},{1... | collective-permute-start | bytes 2359304 | tf_op jit(solution)/shard_map/ppermute | solution.py:24
  77.9 3.7 %copy-start.16 = (bf16[384,768]{1,0:T(8,128)(2,1)S(1)}, bf16[384,768]{1,0:T(8,128)(2,1)}, u32[]{:S(2)}) copy-start(bf16[384,768]{1,0:T(8,128)(2,1)} %copy-done.15) | copy-start | bytes 1769476
  79.2 70.0 %collective-permute-start.1 = (bf16[2,4,384,256]{3,2,1,0:T(8,128)(2,1)}, bf16[2,4,384,256]{3,2,1,0:T(8,128)(2,1)}, u32[]{:S(2)}, u32[]{:S(2)}) collective-permute-start(bf16[2,4,384,256]{3,2,1,0:T(8,128)(2,1)} %pad_maximum_fusion), channel_id=1, source_target_pairs={{0,8},{4,12},{8,0},{12,4},{1,9},{5,13},{9,1},{13,5},{2,10},{6,14},... | collective-permute-start | bytes 4718600 | tf_op jit(solution)/shard_map/ppermute | solution.py:24
  152.7 0.7 copy-start.6
  157.7 0.9 copy-start.7
  158.6 0.7 copy-start.6
  163.6 0.9 copy-start.7
  164.5 32.5 %copy-start.3 = (bf16[384,384]{1,0:T(8,128)(2,1)S(1)}, bf16[384,384]{1,0:T(8,128)(2,1)}, u32[]{:S(2)}) copy-start(bf16[384,384]{1,0:T(8,128)(2,1)} %copy-done.2) | copy-start | bytes 884740
  164.5 32.5 %copy-start.5 = (bf16[384,384]{1,0:T(8,128)(2,1)S(1)}, bf16[384,384]{1,0:T(8,128)(2,1)}, u32[]{:S(2)}) copy-start(bf16[384,384]{1,0:T(8,128)(2,1)} %copy-done.4) | copy-start | bytes 884740
  166.8 77.7 %all-reduce.6.cloned.1.call-start = ((), (), s32[]{:S(2)}) async-start(), calls=%async_computation.1 | async-start | bytes 1179648 | tf_op jit(solution)/shard_map/psum | solution.py:170
  198.4 1.7 copy-start.10
  200.3 0.7 copy-start.8
  205.2 0.9 copy-start.9
  206.2 0.7 copy-start.8
  211.1 0.9 copy-start.9
  212.0 2.3 slice-start
  214.3 30.3 %copy-start.11 = (bf16[384,768]{1,0:T(8,128)(2,1)S(1)}, bf16[384,768]{1,0:T(8,128)(2,1)}, u32[]{:S(2)}) copy-start(bf16[384,768]{1,0:T(8,128)(2,1)} %copy-done.10) | copy-start | bytes 1769476
  246.3 5.0 %collective-permute-start.2 = (bf16[1,66,256]{2,1,0:T(8,128)(2,1)S(1)}, bf16[1,66,256]{2,1,0:T(8,128)(2,1)S(1)}, u32[]{:S(2)}, u32[]{:S(2)}) collective-permute-start(bf16[1,66,256]{2,1,0:T(8,128)(2,1)S(1)} %get-tuple-element.216), channel_id=1, source_target_pairs={{0,4},{4,8},{8,12},{1,5},{5,9},{9,13},{2,6},{6,10},{10,14},{3,7},{... | collective-permute-start | bytes 101384 | tf_op jit(solution)/shard_map/ppermute | solution.py:43
  249.7 5.9 %collective-permute-start.3 = (bf16[1,66,256]{2,1,0:T(8,128)(2,1)S(1)}, bf16[1,66,256]{2,1,0:T(8,128)(2,1)S(1)}, u32[]{:S(2)}, u32[]{:S(2)}) collective-permute-start(bf16[1,66,256]{2,1,0:T(8,128)(2,1)S(1)} %get-tuple-element.215), channel_id=1, source_target_pairs={{4,0},{8,4},{12,8},{5,1},{9,5},{13,9},{6,2},{10,6},{14,10},{7,3},{... | collective-permute-start | bytes 101384 | tf_op jit(solution)/shard_map/ppermute | solution.py:45
Sparse Core Ops, SparseCore 0:
  10.1 29.8 all-gather.2
  167.0 30.0 all-reduce.3
  214.4 30.0 all-reduce.5
